TPU v7x, 256 devices: a whole 4x4x8 slice. The times are simulated.
256 devices in a mesh: view: 8 (over z), gx: 4 (over x), gy: 8 (over y, core).
Axes of the slice: x: 4, y: 4, z: 8, core: 2. Of those that a mesh axis runs over, the one named last changes fastest.
Arguments:
- velocity: float32 [3, 128, 1024, 1024], P(None, 'gx', 'gy', 'view'), may hold values from -6 to 6
- occupied: int32 [16, 128, 8], P('gx', 'gy', 'view'), may hold values 0 or 1
- q_floor: float32 [1], replicated, may hold values from -1 to 0
- q_span: float32 [1], replicated, may hold values from 1 to 4
Outputs:
- image: float32 [4, 8, 4, 32, 128], P('gx', 'gy', None, 'view')
All inputs are finite; a program needn't handle non-finite values. No bound on the sum of `occupied` on one device may be relied on, other than what follows from the above.
Results may differ from a plain program's by a relative error of at most 0.0003.
Values sent between devices are 32-bit elements; how exact they have to be, the bound alone decides.
A program may use at most 128 MiB of HBM per device.

v0:
```python
import jax
import jax.numpy as jnp
from jax import lax
from jax.sharding import PartitionSpec as P

SUB = 8


def extended(cells, sides, width):
    for axis, dim in sides:
        count = lax.axis_size(axis)
        head = lax.slice_in_dim(cells, 0, width, axis=dim)
        tail = lax.slice_in_dim(cells, cells.shape[dim] - width, cells.shape[dim], axis=dim)
        cells = jnp.concatenate(
            [
                lax.ppermute(tail, axis, [(i, (i + 1) % count) for i in range(count)]),
                cells,
                lax.ppermute(head, axis, [((i + 1) % count, i) for i in range(count)]),
            ],
            axis=dim,
        )
    return cells


def derivative(padded_field, direction):
    length_inner = padded_field.shape[direction] - 4

    def shifted(offset):
        return lax.slice_in_dim(padded_field, offset, offset + length_inner, axis=direction)

    return (shifted(0) - 8.0 * shifted(1) + 8.0 * shifted(3) - shifted(4)) / 12.0


def criterion(padded_sets):
    gradient = [
        [derivative(padded_sets[column][component], column) for column in range(3)]
        for component in range(3)
    ]
    diagonal_part = (
        gradient[0][0] * gradient[0][0]
        + gradient[1][1] * gradient[1][1]
        + gradient[2][2] * gradient[2][2]
    )
    cross_part = (
        gradient[0][1] * gradient[1][0]
        + gradient[0][2] * gradient[2][0]
        + gradient[1][2] * gradient[2][1]
    )
    return -0.5 * diagonal_part - cross_part


def local(velocity, occupied, q_floor, q_span):
    brick_x, brick_y, brick_z = (velocity.shape[1], velocity.shape[2], velocity.shape[3])
    view_count = lax.axis_size("view")
    density = 5.0 / (brick_z * view_count)
    pad_across = extended(velocity, (("gx", 1),), 2)
    pad_down = extended(velocity, (("gy", 2),), 2)
    pad_depth = extended(velocity, (("view", 3),), 2)
    padded_sets = (pad_across, pad_down, pad_depth)
    qvalue = criterion(padded_sets)
    occupancy = occupied[:, :, 0].astype(jnp.float32)
    shade_level = jnp.clip((qvalue - q_floor[0]) / q_span[0], 0.0, 1.0)
    shade_level = shade_level.reshape(brick_x // SUB, SUB, brick_y // SUB, SUB, brick_z)
    shade_level = (shade_level * occupancy[:, None, :, None, None]).reshape(
        brick_x, brick_y, brick_z
    )
    optical = density * shade_level
    coverage = 1.0 - jnp.exp(-optical)
    steps_row = lax.broadcasted_iota(jnp.int32, (brick_z, brick_z), 0)
    steps_col = lax.broadcasted_iota(jnp.int32, (brick_z, brick_z), 1)
    strict_upper = (steps_row < steps_col).astype(jnp.float32)
    before = jnp.dot(
        optical.reshape(brick_x * brick_y, brick_z), strict_upper, precision=lax.Precision.HIGHEST
    )
    weight = jnp.exp(-before.reshape(brick_x, brick_y, brick_z)) * coverage
    red = jnp.sum(weight * shade_level, axis=-1)
    green = jnp.sum(weight * 4.0 * shade_level * (1.0 - shade_level), axis=-1)
    blue = jnp.sum(weight * (1.0 - shade_level), axis=-1)
    through = jnp.exp(-jnp.sum(optical, axis=-1))
    partial_value = jnp.stack([red, green, blue, through], axis=0)
    block_rows = brick_x // view_count
    holding = partial_value.reshape(4, view_count, block_rows, brick_y)
    arrived = lax.all_to_all(holding, "view", split_axis=1, concat_axis=1, tiled=True)
    passing = arrived[3:]
    running = jnp.cumprod(passing, axis=1)
    ahead_pass = jnp.concatenate([jnp.ones_like(passing[:, :1]), running[:, :-1]], axis=1)
    colour_sum = jnp.sum(ahead_pass * arrived[:3], axis=1, keepdims=True)
    holding = jnp.concatenate([colour_sum, running[:, -1:]], axis=0)
    finished = jnp.concatenate([holding[:3], 1.0 - holding[3:]], axis=0)
    return finished.reshape(1, 1, 4, block_rows, brick_y)


def solution(mesh):
    placed = (P(None, "gx", "gy", "view"), P("gx", "gy", "view"), P(), P())
    return jax.shard_map(
        local,
        mesh=mesh,
        in_specs=placed,
        out_specs=P("gx", "gy", None, "view", None),
        check_vma=False,
    )
```

profile of v0, /device:TPU:16, one launch (start us, length us, event | category | flops | bytes accessed | tf_op | source)
XLA Modules:
  0.0 138.8 jit_solution(3339839494912392464)
XLA Ops:
  0.0 1.2 fusion.76
  1.2 0.0 collective-permute-start.3
  1.3 0.0 copy-start
  1.3 0.5 collective-permute-start.2
  1.8 6.6 %copy.27 = f32[3,32,128,128]{2,3,1,0:T(8,128)} copy(f32[3,32,128,128]{3,2,1,0:T(8,128)} %param.4) | data formatting | bytes 12582912 | tf_op args[0]
  8.4 1.9 %fusion.75 = (f32[3,32,128,2]{2,3,1,0:T(2,128)}, f32[3,32,128,2]{2,3,1,0:T(2,128)}) fusion(f32[3,32,128,128]{2,3,1,0:T(8,128)} %copy.27), kind=kLoop, calls=%fused_computation.133 | loop fusion | bytes 393216 | tf_op jit(solution)/shard_map/slice | solution.py:13
  10.3 5.9 %collective-permute-start.5 = (f32[3,32,128,2]{2,3,1,0:T(2,128)}, f32[3,32,128,2]{2,3,1,0:T(2,128)}, u32[]{:S(2)}, u32[]{:S(2)}) collective-permute-start(f32[3,32,128,2]{2,3,1,0:T(2,128)} %get-tuple-element.18), channel_id=1, source_target_pairs={{32,0},{64,32},{96,64},{128,96},{160,128},{192,160},{224,192},{0,2... | collective-permute-start | bytes 294920 | tf_op jit(solution)/shard_map/ppermute | solution.py:18
  16.1 2.1 %fusion.74 = (f32[3,2,128,128]{2,3,1,0:T(8,128)}, f32[3,2,128,128]{2,3,1,0:T(8,128)}) fusion(f32[3,32,128,128]{2,3,1,0:T(8,128)} %copy.27), kind=kLoop, calls=%fused_computation.132 | loop fusion | bytes 1572864 | tf_op jit(solution)/shard_map/slice | solution.py:13
  18.2 2.8 %collective-permute-start.1 = (f32[3,2,128,128]{2,3,1,0:T(8,128)}, f32[3,2,128,128]{2,3,1,0:T(8,128)S(1)}, u32[]{:S(2)}, u32[]{:S(2)}) collective-permute-start(f32[3,2,128,128]{2,3,1,0:T(8,128)} %get-tuple-element.16), channel_id=1, source_target_pairs={{8,0},{16,8},{24,16},{0,24},{9,1},{17,9},{25,17},{1,25},{10,2},{18... | collective-permute-start | bytes 1179656 | tf_op jit(solution)/shard_map/ppermute | solution.py:18
  21.0 0.1 mul.162
  21.1 0.1 mul.163
  22.5 0.3 collective-permute-start
  22.8 3.9 %copy.35 = f32[3,32,2,128]{2,3,1,0:T(8,128)} copy(f32[3,32,2,128]{3,1,2,0:T(8,128)S(1)} %collective-permute-done.3) | data formatting | bytes 196608 | tf_op jit(solution)/shard_map/ppermute | solution.py:18
  26.7 0.0 collective-permute-done.2
  26.7 4.0 %copy.33 = f32[3,32,2,128]{2,3,1,0:T(8,128)} copy(f32[3,32,2,128]{3,1,2,0:T(8,128)S(1)} %collective-permute-done.2) | data formatting | bytes 196608 | tf_op jit(solution)/shard_map/ppermute | solution.py:16
  30.8 14.8 %pad_maximum_fusion = f32[3,32,132,128]{2,3,1,0:T(8,128)} fusion(f32[3,32,2,128]{2,3,1,0:T(8,128)} %copy.35, f32[3,32,128,128]{2,3,1,0:T(8,128)} %copy.27, f32[3,32,2,128]{2,3,1,0:T(8,128)} %copy.33), kind=kLoop, calls=%fused_computation.10 | loop fusion | flops 3244032 | bytes 12976128 | tf_op jit(solution)/shard_map/concatenate | solution.py:14
  45.5 9.7 %slice_bitcast_fusion.2 = (f32[32,132,128]{1,2,0:T(8,128)}, f32[32,132,128]{1,2,0:T(8,128)}, f32[32,132,128]{1,2,0:T(8,128)}) fusion(f32[3,32,132,128]{2,3,1,0:T(8,128)} %pad_maximum_fusion), kind=kLoop, calls=%fused_computation.24 | loop fusion | bytes 12976128 | tf_op jit(solution)/shard_map/squeeze | solution.py:36
  55.3 0.0 collective-permute-done.5
  55.3 2.0 %pad_maximum_fusion.1 = f32[3,32,128,132]{2,3,1,0:T(8,128)S(1)} fusion(f32[3,32,128,2]{2,3,1,0:T(2,128)} %collective-permute-done.5, f32[3,32,128,128]{2,3,1,0:T(8,128)S(1)} %bitcast.112, f32[3,32,128,2]{2,3,1,0:T(2,128)} %collective-permute-done.4), kind=kLoop, calls=%fused_computation.11 | loop fusion | flops 3244032 | bytes 12976128 | tf_op jit(solution)/shard_map/concatenate | solution.py:14
  57.3 2.5 %slice_bitcast_fusion.5 = (f32[32,128,132]{1,2,0:T(8,128)S(1)}, f32[32,128,132]{1,2,0:T(8,128)}, f32[32,128,132]{1,2,0:T(8,128)}) fusion(f32[3,32,128,132]{2,3,1,0:T(8,128)S(1)} %pad_maximum_fusion.1), kind=kLoop, calls=%fused_computation.27 | loop fusion | bytes 12976128 | tf_op jit(solution)/shard_map/squeeze | solution.py:36
  59.8 32.3 %fusion.66.clone.5 = f32[32,128,128]{1,2,0:T(8,128)} fusion(f32[32,128]{1,0:T(8,128)S(1)} %mul.163, f32[]{:T(128)} %bitcast.110, f32[]{:T(128)} %bitcast.108, f32[32,132,128]{1,2,0:T(8,128)} %get-tuple-element.10, f32[32,128,132]{1,2,0:T(8,128)} %get-tuple-element.13, f32[3,2,128,128]{2,3,1,0:T(8,128)S(1)} %collective-permute-done.1, ...), kind=kLoop, calls=%fused_computation.118.clone.clone.clone.clone.clone.2 | loop fusion | flops 43515904 | bytes 59523080 | tf_op jit(solution)/shard_map/reduce_sum | solution.py:76
  92.1 33.2 %multiply_reduce_fusion.2 = (f32[32,128]{1,0:T(8,128)S(1)}, f32[32,128]{1,0:T(8,128)S(1)}, f32[32,128]{1,0:T(8,128)S(1)}, f32[32,128]{1,0:T(8,128)S(1)}) fusion(f32[32,128]{1,0:T(8,128)S(1)} %mul.163, f32[]{:T(128)} %bitcast.109, f32[]{:T(128)} %bitcast.107, f32[32,132,128]{1,2,0:T(8,128)} %get-tuple-element.10, f32[32,128,132]{1,2,0:T(8,128)} %get-tuple-element.13, ...), kind=kOutput, calls=%fused_computation.113 | convolution fusion | flops 856162304 | bytes 59588616 | tf_op jit(solution)/shard_map/dot_general | solution.py:72
  125.3 12.8 %all_to_all.5 = f32[4,8,4,128]{3,2,0,1:T(4,128)S(1)} all-to-all(f32[4,8,4,128]{3,2,0,1:T(4,128)S(1)} %pad_maximum_fusion.4), channel_id=1, replica_groups=mesh['view'=8,'gx'=4,'gy'=8] {'view'}, dimensions={1} | all-to-all | bytes 131072 | tf_op jit(solution)/shard_map/all_to_all | solution.py:83
  138.2 0.6 maximum_bitcast_fusion
  (21 shorter events, 0.1 us)
Async XLA Ops:
  1.2 21.3 %collective-permute-start.3 = (f32[3,32,2,128]{3,1,2,0:T(8,128)S(1)}, f32[3,32,2,128]{3,1,2,0:T(8,128)S(1)}, u32[]{:S(2)}, u32[]{:S(2)}) collective-permute-start(f32[3,32,2,128]{3,1,2,0:T(8,128)S(1)} %copy.42), channel_id=1, source_target_pairs={{1,0},{2,1},{3,2},{4,3},{5,4},{6,5},{7,6},{0,7},{9,8},{10,9},{11,1... | collective-permute-start | bytes 294920 | tf_op jit(solution)/shard_map/ppermute | solution.py:18
  1.3 19.7 %copy-start = (s32[4,16,1]{1,2,0:T(1,128)S(1)}, s32[4,16,1]{1,2,0:T(1,128)}, u32[]{:S(2)}) copy-start(s32[4,16,1]{1,2,0:T(1,128)} %param.5) | copy-start | bytes 772
  1.3 25.5 %collective-permute-start.2 = (f32[3,32,2,128]{3,1,2,0:T(8,128)S(1)}, f32[3,32,2,128]{3,1,2,0:T(8,128)S(1)}, u32[]{:S(2)}, u32[]{:S(2)}) collective-permute-start(f32[3,32,2,128]{3,1,2,0:T(8,128)S(1)} %copy.41), channel_id=1, source_target_pairs={{0,1},{1,2},{2,3},{3,4},{4,5},{5,6},{6,7},{7,0},{8,9},{9,10},{10,1... | collective-permute-start | bytes 294920 | tf_op jit(solution)/shard_map/ppermute | solution.py:16
  10.3 45.0 %collective-permute-start.5 = (f32[3,32,128,2]{2,3,1,0:T(2,128)}, f32[3,32,128,2]{2,3,1,0:T(2,128)}, u32[]{:S(2)}, u32[]{:S(2)}) collective-permute-start(f32[3,32,128,2]{2,3,1,0:T(2,128)} %get-tuple-element.18), channel_id=1, source_target_pairs={{32,0},{64,32},{96,64},{128,96},{160,128},{192,160},{224,192},{0,2... | collective-permute-start | bytes 294920 | tf_op jit(solution)/shard_map/ppermute | solution.py:18
  16.1 39.1 %collective-permute-start.4 = (f32[3,32,128,2]{2,3,1,0:T(2,128)}, f32[3,32,128,2]{2,3,1,0:T(2,128)}, u32[]{:S(2)}, u32[]{:S(2)}) collective-permute-start(f32[3,32,128,2]{2,3,1,0:T(2,128)} %get-tuple-element.17), channel_id=1, source_target_pairs={{0,32},{32,64},{64,96},{96,128},{128,160},{160,192},{192,224},{224... | collective-permute-start | bytes 294920 | tf_op jit(solution)/shard_map/ppermute | solution.py:16
  18.2 41.6 %collective-permute-start.1 = (f32[3,2,128,128]{2,3,1,0:T(8,128)}, f32[3,2,128,128]{2,3,1,0:T(8,128)S(1)}, u32[]{:S(2)}, u32[]{:S(2)}) collective-permute-start(f32[3,2,128,128]{2,3,1,0:T(8,128)} %get-tuple-element.16), channel_id=1, source_target_pairs={{8,0},{16,8},{24,16},{0,24},{9,1},{17,9},{25,17},{1,25},{10,2},{18... | collective-permute-start | bytes 1179656 | tf_op jit(solution)/shard_map/ppermute | solution.py:18
  22.5 37.2 %collective-permute-start = (f32[3,2,128,128]{2,3,1,0:T(8,128)}, f32[3,2,128,128]{2,3,1,0:T(8,128)}, u32[]{:S(2)}, u32[]{:S(2)}) collective-permute-start(f32[3,2,128,128]{2,3,1,0:T(8,128)} %get-tuple-element.15), channel_id=1, source_target_pairs={{0,8},{8,16},{16,24},{24,0},{1,9},{9,17},{17,25},{25,1},{2,10},{10... | collective-permute-start | bytes 1179656 | tf_op jit(solution)/shard_map/ppermute | solution.py:16
  26.7 28.5 %slice-start = ((s8[6291456]{0:T(1024)(128)(4,1)}), s8[2097152]{0:T(1024)(128)(4,1)S(1)}, s32[]{:S(2)}) async-start(s8[6291456]{0:T(1024)(128)(4,1)} %bitcast.111), calls=%async_computation.1 | async-start | bytes 4194304
  30.8 24.5 %slice-start.1 = ((s8[6291456]{0:T(1024)(128)(4,1)}), s8[4194304]{0:T(1024)(128)(4,1)S(1)}, s32[]{:S(2)}) async-start(s8[6291456]{0:T(1024)(128)(4,1)} %bitcast.111), calls=%async_computation.2 | async-start | bytes 8388608
where the time goes:
time: 141 us; the launch traced here: 139 us
  other arithmetic  49.8 us (35%)
  matrix products  33.2 us (24%)
  local copies, waits for them, and re-layouts  32.2 us (23%)
  blocking collectives  12.8 us (9%)
  starting transfers between devices  9.4 us (7%)
  between operations  1.44 us (1%)
    dot_general x1, matrix products, local(): jnp.dot(optical.reshape(brick_x * brick_y, brick_z), strict_upper, precis...  33.2 us
    reduce_sum x1, other arithmetic, local(): red = jnp.sum(weight * shade_level, axis=-1)  32.3 us
    concatenate x2, other arithmetic, extended(): jnp.concatenate([lax.ppermute(tail, axis, [(i, (i + 1) % count) for i in...  16.8 us
    all_to_all x1, blocking collectives, local(): lax.all_to_all(holding, 'view', split_axis=1, concat_axis=1, tiled=True)  12.8 us
    squeeze x2, local copies, waits for them, and re-layouts, criterion(): padded_sets[column][component]  12.2 us
    ppermute x3, starting transfers between devices, extended(): lax.ppermute(head, axis, [((i + 1) % count, i) for i in range(count)])  8.63 us
    unnamed x9, local copies, waits for them, and re-layouts  6.67 us
    slice x3, local copies, waits for them, and re-layouts, extended(): lax.slice_in_dim(cells, cells.shape[dim] - width, cells.shape[dim], axis=...  5.13 us
  transfers between devices with their start and end apart: 6, of which 0 were waited for; matrix products, arithmetic and copies ran while one was open for 34% of the time, Pallas kernels for 0%

commit v1 on v0

v1 whole, which is shorter than its diff:
```python
import functools
import math

import jax
import jax.numpy as jnp
from jax import lax
from jax.experimental import pallas as pl
from jax.experimental.pallas import tpu as pltpu
from jax.sharding import PartitionSpec as P

MESH = pl.DeviceIdType.MESH
SUB = 8
LANES = 128
ROWS = 4
VIEW = 8


def stencil(a, b, c, d):
    return (c - b) - 0.125 * (d - a)


def kernel(
    vel, occ, q_floor, q_span, out,
    cells, packed, send_l, send_r, recv_l, recv_r, edge, split, lower, trans, gain, parts, arrived,
    load_sem, halo_send, halo_recv, z_send, z_recv, part_send, part_recv,
):
    v = lax.axis_index("view")
    gx = lax.axis_index("gx")
    gy = lax.axis_index("gy")
    n_gx, n_gy = lax.axis_size("gx"), lax.axis_size("gy")
    v_next, v_prev = lax.rem(v + 1, VIEW), lax.rem(v + VIEW - 1, VIEW)
    x_next, x_prev = lax.rem(gx + 1, n_gx), lax.rem(gx + n_gx - 1, n_gx)
    y_next, y_prev = lax.rem(gy + 1, n_gy), lax.rem(gy + n_gy - 1, n_gy)

    loads = []
    for g in range(2):
        for c in range(3):
            load = pltpu.make_async_copy(
                vel.at[c, pl.ds(16 * g, 16)],
                cells.at[c, pl.ds(2 + 16 * g, 16), pl.ds(8, 128)],
                load_sem.at[g, c],
            )
            load.start()
            loads.append(load)

    barrier = pltpu.get_barrier_semaphore()
    for target in ({"gx": x_next}, {"gx": x_prev}, {"gy": y_next}, {"gy": y_prev}):
        pl.semaphore_signal(barrier, inc=1, device_id=target, device_id_type=MESH)
    for step in range(1, VIEW):
        pl.semaphore_signal(
            barrier, inc=1, device_id={"view": lax.rem(v + step, VIEW)}, device_id_type=MESH
        )
    pl.semaphore_wait(barrier, 4 + VIEW - 1)

    halos = []

    def send_halo(number, src, dst, target):
        copy = pltpu.make_async_remote_copy(
            src_ref=src, dst_ref=dst, send_sem=halo_send.at[number], recv_sem=halo_recv.at[number],
            device_id=target, device_id_type=MESH,
        )
        copy.start()
        halos.append(copy)

    body = pl.ds(8, 128)
    send_halo(0, vel.at[:, pl.ds(0, 2)], cells.at[:, pl.ds(34, 2), body], {"gx": x_prev})
    send_halo(1, vel.at[:, pl.ds(30, 2)], cells.at[:, pl.ds(0, 2), body], {"gx": x_next})
    send_halo(2, vel.at[:, :, pl.ds(0, 2)], cells.at[:, pl.ds(2, 32), pl.ds(136, 2)], {"gy": y_prev})
    send_halo(3, vel.at[:, :, pl.ds(126, 2)], cells.at[:, pl.ds(2, 32), pl.ds(6, 2)], {"gy": y_next})

    lane = lax.broadcasted_iota(jnp.int32, (8, LANES), 1)
    slot = lane % 8
    block = lane // 8
    row_id = lax.broadcasted_iota(jnp.int32, (256, 256), 0)
    col_id = lax.broadcasted_iota(jnp.int32, (256, 256), 1)
    depth_of = col_id % LANES
    chosen = ((row_id < LANES) & (depth_of < row_id)) | (depth_of == row_id - LANES)
    lower[...] = chosen.astype(jnp.float32).astype(jnp.bfloat16)

    def pack(g):
        bits = [(block // (1 << n)) % 2 == 1 for n in range(4)]

        @pl.loop(0, 16)
        def _(t):
            rows = pl.ds(pl.multiple_of(8 + 8 * t, 8), 8)
            own = pl.ds(pl.multiple_of(8 * t, 8), 8)
            left = jnp.zeros((8, LANES), jnp.float32)
            right = jnp.zeros((8, LANES), jnp.float32)
            for c in range(3):
                terms = [
                    pltpu.roll(cells[c, 2 + 16 * g + x, rows], (8 * x + 4) % LANES, 1)
                    for x in range(16)
                ]
                for n in range(4):
                    terms = [
                        jnp.where(bits[n], terms[2 * i + 1], terms[2 * i])
                        for i in range(len(terms) // 2)
                    ]
                packed[g, c, own] = terms[0]
                here = slot // 2 == c
                left = jnp.where(here, pltpu.roll(terms[0], (2 * c - 4) % LANES, 1), left)
                right = jnp.where(here, pltpu.roll(terms[0], (2 * c - 2) % LANES, 1), right)
            send_l[g, own] = left
            send_r[g, own] = right

    z_copies = []
    for g in range(2):
        for c in range(3):
            loads[3 * g + c].wait()
        pack(g)
        for side, (src, dst, target) in enumerate(
            ((send_l, recv_l, {"view": v_prev}), (send_r, recv_r, {"view": v_next}))
        ):
            copy = pltpu.make_async_remote_copy(
                src_ref=src.at[g], dst_ref=dst.at[g], send_sem=z_send.at[g, side],
                recv_sem=z_recv.at[g, side], device_id=target, device_id_type=MESH,
            )
            copy.start()
            z_copies.append(copy)

    for g in range(2):
        for copy in z_copies[2 * g : 2 * g + 2]:
            copy.wait_recv()

        @pl.loop(0, 16)
        def _(t):
            own = pl.ds(pl.multiple_of(8 * t, 8), 8)
            after, before = recv_l[g, own], recv_r[g, own]
            for c in range(3):
                mine = packed[g, c, own]
                upper = jnp.where(slot // 2 == 2, pltpu.roll(after, (4 - 2 * c) % LANES, 1), mine)
                under = jnp.where(slot // 2 == 1, pltpu.roll(before, (2 - 2 * c) % LANES, 1), mine)

                def along(w):
                    return stencil(
                        pltpu.roll(w, 2, 1), pltpu.roll(w, 1, 1),
                        pltpu.roll(w, LANES - 1, 1), pltpu.roll(w, LANES - 2, 1),
                    )

                edge[g, c, own] = jnp.where(slot < 4, along(upper), along(under))

    for copy in halos:
        copy.wait_recv()

    unit = -(5.0 / (LANES * VIEW)) * math.log2(math.e)
    slope = -unit / (4.5 * q_span[0])
    shift = -unit * q_floor[0] / q_span[0]

    rim = (lane < 2) | (lane >= LANES - 2)
    rim16 = jnp.concatenate([rim, rim], axis=0)

    def level_of(b, k, t):
        x = 4 * b + k + 2
        top = 8 + 16 * t
        g = b // 4
        turn = 124 - 32 * (b % 4) - 8 * k
        grad = []
        for c in range(3):
            def at(dx, dy):
                return cells[c, x + dx, pl.ds(top + dy, 16)]

            mine = at(0, 0)
            across = stencil(at(-2, 0), at(-1, 0), at(1, 0), at(2, 0))
            down = stencil(at(0, -2), at(0, -1), at(0, 1), at(0, 2))
            ahead = pltpu.roll(mine, LANES - 2, 1) - mine
            deep = pltpu.roll(ahead, 1, 1) - 0.125 * (ahead + pltpu.roll(ahead, 2, 1))
            ends = pltpu.roll(edge[g, c, pl.ds(16 * t, 16)], turn, 1)
            deep = jnp.where(rim16, ends, deep)
            grad.append((across, down, deep))
        squares = grad[0][0] * grad[0][0] + grad[1][1] * grad[1][1] + grad[2][2] * grad[2][2]
        cross = grad[0][1] * grad[1][0] + grad[0][2] * grad[2][0] + grad[1][2] * grad[2][1]
        total = (squares + cross) + cross
        factors = []
        for half in range(2):
            keep = occ[b // 2, 0, 2 * t + half].astype(jnp.float32)
            factors.append((slope * keep, shift * keep))
        m = jnp.concatenate([jnp.full((8, LANES), f[0], jnp.float32) for f in factors], axis=0)
        s = jnp.concatenate([jnp.full((8, LANES), f[1], jnp.float32) for f in factors], axis=0)
        return jnp.maximum(jnp.minimum(total * m + s, 0.0), unit)

    def block_of(step):
        far = 4 + jnp.where(step % 2 == 1, -1, 1) * ((step + 1) // 2)
        return (v + far) % VIEW

    def do_block(step):
        b = block_of(step)
        for k in range(ROWS):
            for t in range(8):
                lev = level_of(b, k, t)
                high = lev.astype(jnp.bfloat16)
                low = (lev - high.astype(jnp.float32)).astype(jnp.bfloat16)
                here = pl.ds(128 * (k % 2) + 16 * t, 16)
                split[k // 2, here, pl.ds(0, LANES)] = high
                split[k // 2, here, pl.ds(LANES, LANES)] = low
        for pair in range(2):
            turned = lax.dot_general(
                lower[...], split[pair], (((1,), (1,)), ((), ())),
                preferred_element_type=jnp.float32,
            )
            first = jnp.zeros((8, 256), jnp.float32)
            second = jnp.zeros((8, 256), jnp.float32)
            for z in range(16):
                passing = jnp.exp2(turned[8 * z : 8 * z + 8])
                lev = turned[128 + 8 * z : 136 + 8 * z]
                left = passing * jnp.exp2(lev)
                one = (passing - left) * lev
                first = first + one
                second = second + one * lev
            rows = [
                jnp.sum(first, axis=0, keepdims=True),
                jnp.sum(second, axis=0, keepdims=True),
                left[7:8],
            ]
            for q in range(3):
                for k in range(2):
                    parts[step, pl.ds(4 * q + 2 * pair + k, 1)] = rows[q][:, 128 * k : 128 * k + 128]
        return b

    def part_copy(step):
        far = 4 + jnp.where(step % 2 == 1, -1, 1) * ((step + 1) // 2)
        return pltpu.make_async_remote_copy(
            src_ref=parts.at[step], dst_ref=arrived.at[v], send_sem=part_send.at[step],
            recv_sem=part_recv.at[step], device_id={"view": (v + far) % VIEW},
            device_id_type=MESH,
        )

    @pl.loop(0, VIEW - 1)
    def _(step):
        do_block(step)
        part_copy(step).start()

    do_block(VIEW - 1)
    arrived[v] = parts[VIEW - 1]

    for step in range(VIEW - 1):
        part_copy(step).wait_recv()

    red = jnp.zeros((ROWS, LANES), jnp.float32)
    green = jnp.zeros((ROWS, LANES), jnp.float32)
    ahead = jnp.ones((ROWS, LANES), jnp.float32)
    for s in range(VIEW):
        red = red + ahead * arrived[s, 0:4]
        green = green + ahead * arrived[s, 4:8]
        ahead = ahead * arrived[s, 8:12]
    red = red * (1.0 / unit)
    green = 4.0 * (red - green * (1.0 / (unit * unit)))
    out[0, 0, 0] = red
    out[0, 0, 1] = green
    out[0, 0, 2] = (1.0 - ahead) - red
    out[0, 0, 3] = 1.0 - ahead

    for copy in halos + z_copies:
        copy.wait_send()
    for step in range(VIEW - 1):
        part_copy(step).wait_send()


def local(velocity, occupied, q_floor, q_span):
    f32, bf16 = jnp.float32, jnp.bfloat16
    smem = pl.BlockSpec(memory_space=pltpu.SMEM)
    return pl.pallas_call(
        kernel,
        out_shape=jax.ShapeDtypeStruct((1, 1, 4, ROWS, LANES), f32),
        in_specs=[pl.BlockSpec(memory_space=pl.ANY), smem, smem, smem],
        out_specs=pl.BlockSpec(memory_space=pltpu.VMEM),
        scratch_shapes=[
            pltpu.VMEM((3, 36, 144, LANES), f32),
            pltpu.VMEM((2, 3, 128, LANES), f32),
            pltpu.VMEM((2, 128, LANES), f32),
            pltpu.VMEM((2, 128, LANES), f32),
            pltpu.VMEM((2, 128, LANES), f32),
            pltpu.VMEM((2, 128, LANES), f32),
            pltpu.VMEM((2, 3, 128, LANES), f32),
            pltpu.VMEM((2, 256, 256), bf16),
            pltpu.VMEM((256, 256), bf16),
            pltpu.VMEM((8, LANES), f32),
            pltpu.VMEM((8, LANES), f32),
            pltpu.VMEM((VIEW, 16, LANES), f32),
            pltpu.VMEM((VIEW, 16, LANES), f32),
            pltpu.SemaphoreType.DMA((2, 3)),
            pltpu.SemaphoreType.DMA((4,)),
            pltpu.SemaphoreType.DMA((4,)),
            pltpu.SemaphoreType.DMA((2, 2)),
            pltpu.SemaphoreType.DMA((2, 2)),
            pltpu.SemaphoreType.DMA((VIEW - 1,)),
            pltpu.SemaphoreType.DMA((VIEW - 1,)),
        ],
        compiler_params=pltpu.CompilerParams(collective_id=0, has_side_effects=True),
    )(velocity, occupied.transpose(0, 2, 1), q_floor, q_span)


def solution(mesh):
    placed = (P(None, "gx", "gy", "view"), P("gx", "gy", "view"), P(), P())
    return jax.shard_map(
        local,
        mesh=mesh,
        in_specs=placed,
        out_specs=P("gx", "gy", None, "view", None),
        check_vma=False,
    )
```

time: 141 us -> 56.7 us (0.40); the launches traced: 139 us -> 56.5 us
  Pallas kernels: 0 us -> 53.9 us
  other arithmetic: 49.8 us -> 0 us
  matrix products: 33.2 us -> 0 us
  local copies, waits for them, and re-layouts: 32.2 us -> 1.3 us
  blocking collectives: 12.8 us -> 0 us
  starting transfers between devices: 9.4 us -> 0 us
    pallas_call x0 -> x1, Pallas kernels: none -> 53.9 us  [local(): pl.pallas_call(kernel, out_shape=jax.ShapeDtypeStruct((1, 1, 4, ROWS, LAN...]
    dot_general x1 -> x0, matrix products: 33.2 us -> none  [local(): jnp.dot(optical.reshape(brick_x * brick_y, brick_z), strict_upper, precis...]
    reduce_sum x2 -> x0, other arithmetic: 32.3 us -> none  [the longest x1 32.3 us: local(): red = jnp.sum(weight * shade_level, axis=-1)]
    concatenate x2 -> x0, other arithmetic: 16.8 us -> none  [extended(): jnp.concatenate([lax.ppermute(tail, axis, [(i, (i + 1) % count) for i in...]
    all_to_all x1 -> x0, blocking collectives: 12.8 us -> none  [local(): lax.all_to_all(holding, 'view', split_axis=1, concat_axis=1, tiled=True)]
    squeeze x2 -> x0, local copies, waits for them, and re-layouts: 12.2 us -> none  [criterion(): padded_sets[column][component]]
    ppermute x6 -> x0, starting transfers between devices: 9.4 us -> none  [the longest x3 8.63 us: extended(): lax.ppermute(head, axis, [((i + 1) % count, i) for i in range(count)])]
    ppermute x2 -> x0, local copies, waits for them, and re-layouts: 7.98 us -> none  [the longest x1 4.04 us: extended(): lax.ppermute(tail, axis, [(i, (i + 1) % count) for i in range(count)])]
  transfers between devices with their start and end apart: 6 -> 0, of which waited for: 0 -> 0; matrix products, arithmetic and copies ran while one was open for 34% -> 0% of each run, Pallas kernels for 0% -> 0%
where the time goes in v1:
time: 56.7 us; the launch traced here: 56.5 us
  Pallas kernels  53.9 us (95%)
  local copies, waits for them, and re-layouts  1.3 us (2%)
  between operations  1.3 us (2%)
    pallas_call x1, Pallas kernels, local(): pl.pallas_call(kernel, out_shape=jax.ShapeDtypeStruct((1, 1, 4, ROWS, LAN...  53.9 us
    unnamed x1, local copies, waits for them, and re-layouts  1.3 us

profile of v1, /device:TPU:16, one launch (start us, length us, event | category | flops | bytes accessed | tf_op | source)
XLA Modules:
  0.0 56.5 jit_solution(9555547309403914297)
XLA Ops:
  1.3 53.9 %shard_map.46 = f32[1,1,4,4,128]{4,3,2,1,0:T(4,128)} custom-call(f32[3,32,128,128]{3,2,1,0:T(8,128)} %vel.1, s32[4,1,16]{2,1,0:T(1,128)} %bitcast.3, f32[1]{0:T(128)S(6)} %copy.7.q_floor, f32[1]{0:T(128)S(6)} %copy.8.q_span), custom_call_target="tpu_custom_call" | custom-call | tf_op jit(solution)/shard_map/pallas_call | solution.py:261
  55.2 1.3 %copy.9 = f32[1,1,4,4,128]{4,3,2,1,0:T(4,128)} copy(f32[1,1,4,4,128]{4,3,2,1,0:T(4,128)} %shard_map.46) | data formatting | bytes 16384

commit v2 on v1

v2 whole, which is shorter than its diff:
```python
import functools
import math

import jax
import jax.numpy as jnp
from jax import lax
from jax.experimental import pallas as pl
from jax.experimental.pallas import tpu as pltpu
from jax.sharding import PartitionSpec as P

MESH = pl.DeviceIdType.MESH
SUB = 8
LANES = 128
ROWS = 4
VIEW = 8


def stencil(a, b, c, d):
    return (c - b) - 0.125 * (d - a)


def kernel(
    vel, occ, q_floor, q_span, out,
    cells, pieces, stencils, send_l, send_r, recv_l, recv_r, deep_ref, split, lower, parts, arrived,
    load_sem, halo_send, halo_recv, z_send, z_recv, part_send, part_recv, ready,
):
    f32, bf16 = jnp.float32, jnp.bfloat16
    v = lax.axis_index("view")
    gx = lax.axis_index("gx")
    gy = lax.axis_index("gy")
    n_gx, n_gy = lax.axis_size("gx"), lax.axis_size("gy")

    def view(step):
        return lax.rem(v + VIEW + step, VIEW)

    x_next, x_prev = lax.rem(gx + 1, n_gx), lax.rem(gx + n_gx - 1, n_gx)
    y_next, y_prev = lax.rem(gy + 1, n_gy), lax.rem(gy + n_gy - 1, n_gy)

    loads = []
    for g in range(2):
        for c in range(3):
            load = pltpu.make_async_copy(
                vel.at[c, pl.ds(16 * g, 16)],
                cells.at[c, pl.ds(2 + 16 * g, 16), pl.ds(8, 128)],
                load_sem.at[g, c],
            )
            load.start()
            loads.append(load)

    barrier = pltpu.get_barrier_semaphore()
    for target in (
        {"gx": x_next}, {"gx": x_prev}, {"gy": y_next}, {"gy": y_prev},
        {"view": view(1)}, {"view": view(-1)},
    ):
        pl.semaphore_signal(barrier, inc=1, device_id=target, device_id_type=MESH)
    pl.semaphore_wait(barrier, 6)

    halos = []

    def send_halo(number, src, dst, target):
        copy = pltpu.make_async_remote_copy(
            src_ref=src, dst_ref=dst, send_sem=halo_send.at[number], recv_sem=halo_recv.at[number],
            device_id=target, device_id_type=MESH,
        )
        copy.start()
        halos.append(copy)

    body = pl.ds(8, 128)
    send_halo(0, vel.at[:, pl.ds(0, 2)], cells.at[:, pl.ds(34, 2), body], {"gx": x_prev})
    send_halo(1, vel.at[:, pl.ds(30, 2)], cells.at[:, pl.ds(0, 2), body], {"gx": x_next})
    send_halo(2, vel.at[:, :, pl.ds(0, 2)], cells.at[:, pl.ds(2, 32), pl.ds(136, 2)], {"gy": y_prev})
    send_halo(3, vel.at[:, :, pl.ds(126, 2)], cells.at[:, pl.ds(2, 32), pl.ds(6, 2)], {"gy": y_next})

    row_id = lax.broadcasted_iota(jnp.int32, (256, 256), 0)
    col_id = lax.broadcasted_iota(jnp.int32, (256, 256), 1)
    depth_of = col_id % LANES
    chosen = ((row_id < LANES) & (depth_of < row_id)) | (depth_of == row_id - LANES)
    lower[...] = chosen.astype(f32).astype(bf16)

    to = lax.broadcasted_iota(jnp.int32, (LANES, LANES), 1)
    row = lax.broadcasted_iota(jnp.int32, (LANES, LANES), 0)

    def weight(gap):
        near = (gap == 1).astype(f32) - (gap == -1).astype(f32)
        far = (gap == 2).astype(f32) - (gap == -2).astype(f32)
        return (near - 0.125 * far).astype(bf16)

    own_weight = weight(row - to)
    halo_at = jnp.where(row % 4 < 2, row % 4 - 2, row % 4 + LANES - 2)
    halo_weight = weight(halo_at - to)
    for c in range(3):
        for n in range(3):
            stencils[c, pl.ds(LANES * n, LANES)] = own_weight
        stencils[c, pl.ds(3 * LANES, LANES)] = jnp.where(
            row // 8 == c, halo_weight, jnp.zeros_like(halo_weight)
        )

    lane = lax.broadcasted_iota(jnp.int32, (16, LANES), 1)
    pair_of = (lane % 8) // 2

    def pack(g):
        @pl.loop(0, 8)
        def _(t):
            rows = pl.ds(pl.multiple_of(8 + 16 * t, 8), 16)
            own = pl.ds(pl.multiple_of(16 * t, 16), 16)
            gathered = [jnp.zeros((16, LANES), f32) for s in range(4)]
            for k in range(4):
                for c in range(3):
                    here = lane // 8 == 4 * k + c
                    for s in range(4):
                        x = 16 * g + 4 * s + k
                        u = cells[c, 2 + x, rows]
                        high = u.astype(bf16)
                        rest = u - high.astype(f32)
                        mid = rest.astype(bf16)
                        low = (rest - mid.astype(f32)).astype(bf16)
                        pieces[c, x, own, pl.ds(0, LANES)] = high
                        pieces[c, x, own, pl.ds(LANES, LANES)] = mid
                        pieces[c, x, own, pl.ds(2 * LANES, LANES)] = low
                        moved = pltpu.roll(u, (32 * k + 8 * c + 4) % LANES, 1)
                        gathered[s] = jnp.where(here, moved, gathered[s])
            left = right = None
            for s in range(4):
                turned = gathered[s] if s == 2 else pltpu.roll(gathered[s], (2 * s - 4) % LANES, 1)
                left = turned if s == 0 else jnp.where(pair_of == s, turned, left)
                right = turned if s == 0 else jnp.where(pair_of == (s + 3) % 4, turned, right)
            send_l[g, own] = left
            send_r[g, own] = right

    z_copies = []
    for g in range(2):
        for c in range(3):
            loads[3 * g + c].wait()
        pack(g)
        for side, (src, dst, step) in enumerate(((send_l, recv_l, -1), (send_r, recv_r, 1))):
            copy = pltpu.make_async_remote_copy(
                src_ref=src.at[g], dst_ref=dst.at[g], send_sem=z_send.at[g, side],
                recv_sem=z_recv.at[g, side], device_id={"view": view(step)}, device_id_type=MESH,
            )
            copy.start()
            z_copies.append(copy)

    for g in range(2):
        for copy in z_copies[2 * g : 2 * g + 2]:
            copy.wait_recv()

        @pl.loop(0, 8)
        def _(t):
            own = pl.ds(pl.multiple_of(16 * t, 16), 16)
            after, before = recv_l[g, own], recv_r[g, own]
            for s in range(4):
                both = jnp.where(pair_of == s, after, before)
                high = both.astype(bf16).astype(f32)
                rest = pltpu.roll(both - high, 4, 1)
                used = (pair_of == s) | (pair_of == (s + 3) % 4)
                halo = jnp.where(used, high, rest)
                for k in range(4):
                    placed = pltpu.roll(halo, (2 - 32 * k - 2 * s) % LANES, 1).astype(bf16)
                    for c in range(3):
                        pieces[c, 16 * g + 4 * s + k, own, pl.ds(3 * LANES, LANES)] = placed

    for step in (2, -2):
        pl.semaphore_signal(ready, inc=1, device_id={"view": view(step)}, device_id_type=MESH)

    for copy in halos[2:]:
        copy.wait_recv()

    unit = -(5.0 / (LANES * VIEW)) * math.log2(math.e)
    slope = -unit / (4.5 * q_span[0])
    shift = -unit * q_floor[0] / q_span[0]

    def level_of(p, k, t):
        x = 2 * p + k + 2
        top = 8 + 16 * t
        grad = []
        for c in range(3):
            def at(dx, dy):
                return cells[c, x + dx, pl.ds(top + dy, 16)]

            across = stencil(at(-2, 0), at(-1, 0), at(1, 0), at(2, 0))
            down = stencil(at(0, -2), at(0, -1), at(0, 1), at(0, 2))
            deep = deep_ref[c, pl.ds(128 * k + 16 * t, 16)]
            grad.append((across, down, deep))
        squares = grad[0][0] * grad[0][0] + grad[1][1] * grad[1][1] + grad[2][2] * grad[2][2]
        cross = grad[0][1] * grad[1][0] + grad[0][2] * grad[2][0] + grad[1][2] * grad[2][1]
        total = (squares + cross) + cross
        factors = []
        for half in range(2):
            keep = occ[p // 4, 0, 2 * t + half].astype(f32)
            factors.append((slope * keep, shift * keep))
        m = jnp.concatenate([jnp.full((8, LANES), f[0], f32) for f in factors], axis=0)
        s = jnp.concatenate([jnp.full((8, LANES), f[1], f32) for f in factors], axis=0)
        return jnp.maximum(jnp.minimum(total * m + s, 0.0), unit)

    def do_pair(p, odd):
        for c in range(3):
            deep_ref[c] = jnp.dot(
                pieces[c, pl.ds(2 * p, 2)].reshape(256, 4 * LANES), stencils[c],
                preferred_element_type=f32,
            )
        for k in range(2):
            for t in range(8):
                lev = level_of(p, k, t)
                high = lev.astype(bf16)
                low = (lev - high.astype(f32)).astype(bf16)
                here = pl.ds(128 * k + 16 * t, 16)
                split[here, pl.ds(0, LANES)] = high
                split[here, pl.ds(LANES, LANES)] = low
        turned = lax.dot_general(
            lower[...], split[...], (((1,), (1,)), ((), ())), preferred_element_type=f32
        )
        first = jnp.zeros((8, 256), f32)
        second = jnp.zeros((8, 256), f32)
        for z in range(16):
            passing = jnp.exp2(turned[8 * z : 8 * z + 8])
            lev = turned[128 + 8 * z : 136 + 8 * z]
            left = passing * jnp.exp2(lev)
            one = (passing - left) * lev
            first = first + one
            second = second + one * lev
        rows = [
            jnp.sum(first, axis=0, keepdims=True),
            jnp.sum(second, axis=0, keepdims=True),
            left[7:8],
        ]
        for q in range(3):
            for k in range(2):
                parts[p // 2, pl.ds(4 * q + 2 * odd + k, 1)] = rows[q][:, 128 * k : 128 * k + 128]

    def part_copy(b, source):
        return pltpu.make_async_remote_copy(
            src_ref=parts.at[b], dst_ref=arrived.at[source], send_sem=part_send.at[b],
            recv_sem=part_recv.at[source], device_id={"view": b}, device_id_type=MESH,
        )

    def hand_over(b):
        @pl.when(b != v)
        def _():
            part_copy(b, v).start()

        @pl.when(b == v)
        def _():
            arrived[v] = parts[b]

    pl.semaphore_wait(ready, 2)

    @pl.loop(1, VIEW - 1)
    def _(b):
        do_pair(2 * b, 0)
        do_pair(2 * b + 1, 1)
        hand_over(b)

    @pl.loop(0, 2)
    def _(i):
        do_pair(1 + 13 * i, 1 - i)

    for copy in halos[:2]:
        copy.wait_recv()

    @pl.loop(0, 2)
    def _(i):
        last = (i + jnp.where(v < 4, 1, 0)) % 2
        do_pair(15 * last, last)
        hand_over(7 * last)

    for step in range(1, VIEW):
        part_copy(view(step), view(step)).wait_recv()

    red = jnp.zeros((ROWS, LANES), f32)
    green = jnp.zeros((ROWS, LANES), f32)
    ahead = jnp.ones((ROWS, LANES), f32)
    for s in range(VIEW):
        red = red + ahead * arrived[s, 0:4]
        green = green + ahead * arrived[s, 4:8]
        ahead = ahead * arrived[s, 8:12]
    red = red * (1.0 / unit)
    green = 4.0 * (red - green * (1.0 / (unit * unit)))
    out[0, 0, 0] = red
    out[0, 0, 1] = green
    out[0, 0, 2] = (1.0 - ahead) - red
    out[0, 0, 3] = 1.0 - ahead

    for copy in halos + z_copies:
        copy.wait_send()
    for step in range(1, VIEW):
        part_copy(view(step), v).wait_send()


def local(velocity, occupied, q_floor, q_span):
    f32, bf16 = jnp.float32, jnp.bfloat16
    smem = pl.BlockSpec(memory_space=pltpu.SMEM)
    return pl.pallas_call(
        kernel,
        out_shape=jax.ShapeDtypeStruct((1, 1, 4, ROWS, LANES), f32),
        in_specs=[pl.BlockSpec(memory_space=pl.ANY), smem, smem, smem],
        out_specs=pl.BlockSpec(memory_space=pltpu.VMEM),
        scratch_shapes=[
            pltpu.VMEM((3, 36, 144, LANES), f32),
            pltpu.VMEM((3, 32, 128, 4 * LANES), bf16),
            pltpu.VMEM((3, 4 * LANES, LANES), bf16),
            pltpu.VMEM((2, 128, LANES), f32),
            pltpu.VMEM((2, 128, LANES), f32),
            pltpu.VMEM((2, 128, LANES), f32),
            pltpu.VMEM((2, 128, LANES), f32),
            pltpu.VMEM((3, 256, LANES), f32),
            pltpu.VMEM((256, 256), bf16),
            pltpu.VMEM((256, 256), bf16),
            pltpu.VMEM((VIEW, 16, LANES), f32),
            pltpu.VMEM((VIEW, 16, LANES), f32),
            pltpu.SemaphoreType.DMA((2, 3)),
            pltpu.SemaphoreType.DMA((4,)),
            pltpu.SemaphoreType.DMA((4,)),
            pltpu.SemaphoreType.DMA((2, 2)),
            pltpu.SemaphoreType.DMA((2, 2)),
            pltpu.SemaphoreType.DMA((VIEW,)),
            pltpu.SemaphoreType.DMA((VIEW,)),
            pltpu.SemaphoreType.REGULAR,
        ],
        compiler_params=pltpu.CompilerParams(collective_id=0, has_side_effects=True),
    )(velocity, occupied.transpose(0, 2, 1), q_floor, q_span)


def solution(mesh):
    placed = (P(None, "gx", "gy", "view"), P("gx", "gy", "view"), P(), P())
    return jax.shard_map(
        local,
        mesh=mesh,
        in_specs=placed,
        out_specs=P("gx", "gy", None, "view", None),
        check_vma=False,
    )
```

time: 56.7 us -> 34.9 us (0.62)
  Pallas kernels: 53.9 us -> 32.1 us
    pallas_call x1, Pallas kernels: 53.9 us -> 32.1 us  [local(): pl.pallas_call(kernel, out_shape=jax.ShapeDtypeStruct((1, 1, 4, ROWS, LAN...]
where the time goes in v2:
time: 34.9 us; the launch traced here: 34.7 us
  Pallas kernels  32.1 us (92%)
  local copies, waits for them, and re-layouts  1.3 us (4%)
  between operations  1.3 us (4%)
    pallas_call x1, Pallas kernels, local(): pl.pallas_call(kernel, out_shape=jax.ShapeDtypeStruct((1, 1, 4, ROWS, LAN...  32.1 us
    unnamed x1, local copies, waits for them, and re-layouts  1.3 us

profile of v2, /device:TPU:16, one launch (start us, length us, event | category | flops | bytes accessed | tf_op | source)
XLA Modules:
  0.0 34.7 jit_solution(3888064878718927177)
XLA Ops:
  1.3 32.1 %shard_map.46 = f32[1,1,4,4,128]{4,3,2,1,0:T(4,128)} custom-call(f32[3,32,128,128]{3,2,1,0:T(8,128)} %vel.1, s32[4,1,16]{2,1,0:T(1,128)} %bitcast.3, f32[1]{0:T(128)S(6)} %copy.7.q_floor, f32[1]{0:T(128)S(6)} %copy.8.q_span), custom_call_target="tpu_custom_call" | custom-call | tf_op jit(solution)/shard_map/pallas_call | solution.py:292
  33.4 1.3 %copy.9 = f32[1,1,4,4,128]{4,3,2,1,0:T(4,128)} copy(f32[1,1,4,4,128]{4,3,2,1,0:T(4,128)} %shard_map.46) | data formatting | bytes 16384

commit v3 on v2

--- a/solution.py
+++ b/solution.py
@@ -20,9 +20,10 @@
 
 
 def kernel(
-    vel, occ, q_floor, q_span, out,
+    vel, occ_in, q_floor_in, q_span_in, out,
     cells, pieces, stencils, send_l, send_r, recv_l, recv_r, deep_ref, split, lower, parts, arrived,
     load_sem, halo_send, halo_recv, z_send, z_recv, part_send, part_recv, ready,
+    occ, q_floor, q_span, small_sem,
 ):
     f32, bf16 = jnp.float32, jnp.bfloat16
     v = lax.axis_index("view")
@@ -47,29 +48,18 @@
             load.start()
             loads.append(load)
 
+    small = []
+    for n, (src, dst) in enumerate(((occ_in, occ), (q_floor_in, q_floor), (q_span_in, q_span))):
+        copy = pltpu.make_async_copy(src, dst, small_sem.at[n])
+        copy.start()
+        small.append(copy)
+
     barrier = pltpu.get_barrier_semaphore()
     for target in (
         {"gx": x_next}, {"gx": x_prev}, {"gy": y_next}, {"gy": y_prev},
         {"view": view(1)}, {"view": view(-1)},
     ):
         pl.semaphore_signal(barrier, inc=1, device_id=target, device_id_type=MESH)
-    pl.semaphore_wait(barrier, 6)
-
-    halos = []
-
-    def send_halo(number, src, dst, target):
-        copy = pltpu.make_async_remote_copy(
-            src_ref=src, dst_ref=dst, send_sem=halo_send.at[number], recv_sem=halo_recv.at[number],
-            device_id=target, device_id_type=MESH,
-        )
-        copy.start()
-        halos.append(copy)
-
-    body = pl.ds(8, 128)
-    send_halo(0, vel.at[:, pl.ds(0, 2)], cells.at[:, pl.ds(34, 2), body], {"gx": x_prev})
-    send_halo(1, vel.at[:, pl.ds(30, 2)], cells.at[:, pl.ds(0, 2), body], {"gx": x_next})
-    send_halo(2, vel.at[:, :, pl.ds(0, 2)], cells.at[:, pl.ds(2, 32), pl.ds(136, 2)], {"gy": y_prev})
-    send_halo(3, vel.at[:, :, pl.ds(126, 2)], cells.at[:, pl.ds(2, 32), pl.ds(6, 2)], {"gy": y_next})
 
     row_id = lax.broadcasted_iota(jnp.int32, (256, 256), 0)
     col_id = lax.broadcasted_iota(jnp.int32, (256, 256), 1)
@@ -127,11 +117,33 @@
             send_l[g, own] = left
             send_r[g, own] = right
 
+    halos = []
+
+    def enter():
+        pl.semaphore_wait(barrier, 6)
+
+
+        def send_halo(number, src, dst, target):
+            copy = pltpu.make_async_remote_copy(
+                src_ref=src, dst_ref=dst, send_sem=halo_send.at[number], recv_sem=halo_recv.at[number],
+                device_id=target, device_id_type=MESH,
+            )
+            copy.start()
+            halos.append(copy)
+
+        body = pl.ds(8, 128)
+        send_halo(0, vel.at[:, pl.ds(0, 2)], cells.at[:, pl.ds(34, 2), body], {"gx": x_prev})
+        send_halo(1, vel.at[:, pl.ds(30, 2)], cells.at[:, pl.ds(0, 2), body], {"gx": x_next})
+        send_halo(2, vel.at[:, :, pl.ds(0, 2)], cells.at[:, pl.ds(2, 32), pl.ds(136, 2)], {"gy": y_prev})
+        send_halo(3, vel.at[:, :, pl.ds(126, 2)], cells.at[:, pl.ds(2, 32), pl.ds(6, 2)], {"gy": y_next})
+
     z_copies = []
     for g in range(2):
         for c in range(3):
             loads[3 * g + c].wait()
         pack(g)
+        if g == 0:
+            enter()
         for side, (src, dst, step) in enumerate(((send_l, recv_l, -1), (send_r, recv_r, 1))):
             copy = pltpu.make_async_remote_copy(
                 src_ref=src.at[g], dst_ref=dst.at[g], send_sem=z_send.at[g, side],
@@ -165,11 +177,14 @@
     for copy in halos[2:]:
         copy.wait_recv()
 
+    for copy in small:
+        copy.wait()
+
     unit = -(5.0 / (LANES * VIEW)) * math.log2(math.e)
-    slope = -unit / (4.5 * q_span[0])
-    shift = -unit * q_floor[0] / q_span[0]
-
-    def level_of(p, k, t):
+    slope = -unit / (4.5 * q_span[0, 0])
+    shift = -unit * q_floor[0, 0] / q_span[0, 0]
+
+    def level_of(p, odd, k, t):
         x = 2 * p + k + 2
         top = 8 + 16 * t
         grad = []
@@ -179,7 +194,7 @@
 
             across = stencil(at(-2, 0), at(-1, 0), at(1, 0), at(2, 0))
             down = stencil(at(0, -2), at(0, -1), at(0, 1), at(0, 2))
-            deep = deep_ref[c, pl.ds(128 * k + 16 * t, 16)]
+            deep = deep_ref[odd, c, pl.ds(128 * k + 16 * t, 16)]
             grad.append((across, down, deep))
         squares = grad[0][0] * grad[0][0] + grad[1][1] * grad[1][1] + grad[2][2] * grad[2][2]
         cross = grad[0][1] * grad[1][0] + grad[0][2] * grad[2][0] + grad[1][2] * grad[2][1]
@@ -192,22 +207,26 @@
         s = jnp.concatenate([jnp.full((8, LANES), f[1], f32) for f in factors], axis=0)
         return jnp.maximum(jnp.minimum(total * m + s, 0.0), unit)
 
-    def do_pair(p, odd):
+    def turn_depth(p, odd):
         for c in range(3):
-            deep_ref[c] = jnp.dot(
+            deep_ref[odd, c] = jnp.dot(
                 pieces[c, pl.ds(2 * p, 2)].reshape(256, 4 * LANES), stencils[c],
                 preferred_element_type=f32,
             )
+
+    def levels(p, odd):
         for k in range(2):
             for t in range(8):
-                lev = level_of(p, k, t)
+                lev = level_of(p, odd, k, t)
                 high = lev.astype(bf16)
                 low = (lev - high.astype(f32)).astype(bf16)
                 here = pl.ds(128 * k + 16 * t, 16)
-                split[here, pl.ds(0, LANES)] = high
-                split[here, pl.ds(LANES, LANES)] = low
+                split[odd, here, pl.ds(0, LANES)] = high
+                split[odd, here, pl.ds(LANES, LANES)] = low
+
+    def finish(p, odd):
         turned = lax.dot_general(
-            lower[...], split[...], (((1,), (1,)), ((), ())), preferred_element_type=f32
+            lower[...], split[odd], (((1,), (1,)), ((), ())), preferred_element_type=f32
         )
         first = jnp.zeros((8, 256), f32)
         second = jnp.zeros((8, 256), f32)
@@ -225,7 +244,7 @@
         ]
         for q in range(3):
             for k in range(2):
-                parts[p // 2, pl.ds(4 * q + 2 * odd + k, 1)] = rows[q][:, 128 * k : 128 * k + 128]
+                parts[p // 2, pl.ds(4 * q + 2 * (p % 2) + k, 1)] = rows[q][:, 128 * k : 128 * k + 128]
 
     def part_copy(b, source):
         return pltpu.make_async_remote_copy(
@@ -244,24 +263,39 @@
 
     pl.semaphore_wait(ready, 2)
 
+    turn_depth(1, 1)
+    levels(1, 1)
+
     @pl.loop(1, VIEW - 1)
     def _(b):
-        do_pair(2 * b, 0)
-        do_pair(2 * b + 1, 1)
-        hand_over(b)
-
-    @pl.loop(0, 2)
-    def _(i):
-        do_pair(1 + 13 * i, 1 - i)
+        turn_depth(2 * b, 0)
+        finish(2 * b - 1, 1)
+        levels(2 * b, 0)
+        turn_depth(2 * b + 1, 1)
+        finish(2 * b, 0)
+        levels(2 * b + 1, 1)
+
+        @pl.when(b > 1)
+        def _():
+            hand_over(b - 1)
+
+    turn_depth(14, 0)
+    finish(13, 1)
+    levels(14, 0)
+    hand_over(6)
+    turn_depth(0, 1)
+    finish(14, 0)
+    turn_depth(15, 0)
 
     for copy in halos[:2]:
         copy.wait_recv()
 
-    @pl.loop(0, 2)
-    def _(i):
-        last = (i + jnp.where(v < 4, 1, 0)) % 2
-        do_pair(15 * last, last)
-        hand_over(7 * last)
+    levels(0, 1)
+    finish(0, 1)
+    hand_over(0)
+    levels(15, 0)
+    finish(15, 0)
+    hand_over(7)
 
     for step in range(1, VIEW):
         part_copy(view(step), view(step)).wait_recv()
@@ -288,11 +322,11 @@
 
 def local(velocity, occupied, q_floor, q_span):
     f32, bf16 = jnp.float32, jnp.bfloat16
-    smem = pl.BlockSpec(memory_space=pltpu.SMEM)
+    here = pl.BlockSpec(memory_space=pltpu.HBM)
     return pl.pallas_call(
         kernel,
         out_shape=jax.ShapeDtypeStruct((1, 1, 4, ROWS, LANES), f32),
-        in_specs=[pl.BlockSpec(memory_space=pl.ANY), smem, smem, smem],
+        in_specs=[here] * 4,
         out_specs=pl.BlockSpec(memory_space=pltpu.VMEM),
         scratch_shapes=[
             pltpu.VMEM((3, 36, 144, LANES), f32),
@@ -302,8 +336,8 @@
             pltpu.VMEM((2, 128, LANES), f32),
             pltpu.VMEM((2, 128, LANES), f32),
             pltpu.VMEM((2, 128, LANES), f32),
-            pltpu.VMEM((3, 256, LANES), f32),
-            pltpu.VMEM((256, 256), bf16),
+            pltpu.VMEM((2, 3, 256, LANES), f32),
+            pltpu.VMEM((2, 256, 256), bf16),
             pltpu.VMEM((256, 256), bf16),
             pltpu.VMEM((VIEW, 16, LANES), f32),
             pltpu.VMEM((VIEW, 16, LANES), f32),
@@ -315,9 +349,13 @@
             pltpu.SemaphoreType.DMA((VIEW,)),
             pltpu.SemaphoreType.DMA((VIEW,)),
             pltpu.SemaphoreType.REGULAR,
+            pltpu.SMEM((4, 1, 16), jnp.int32),
+            pltpu.SMEM((1, 1), f32),
+            pltpu.SMEM((1, 1), f32),
+            pltpu.SemaphoreType.DMA((3,)),
         ],
         compiler_params=pltpu.CompilerParams(collective_id=0, has_side_effects=True),
-    )(velocity, occupied.transpose(0, 2, 1), q_floor, q_span)
+    )(velocity, occupied.transpose(0, 2, 1), q_floor.reshape(1, 1), q_span.reshape(1, 1))
 
 
 def solution(mesh):

time: 34.9 us -> 31.6 us (0.905)
  Pallas kernels: 32.1 us -> 28.9 us
    pallas_call x1, Pallas kernels: 32.1 us -> 28.9 us  [local(): pl.pallas_call(kernel, out_shape=jax.ShapeDtypeStruct((1, 1, 4, ROWS, LAN...]
where the time goes in v3:
time: 31.6 us; the launch traced here: 31.5 us
  Pallas kernels  28.9 us (91%)
  local copies, waits for them, and re-layouts  1.3 us (4%)
  between operations  1.3 us (4%)
    pallas_call x1, Pallas kernels, local(): pl.pallas_call(kernel, out_shape=jax.ShapeDtypeStruct((1, 1, 4, ROWS, LAN...  28.9 us
    unnamed x1, local copies, waits for them, and re-layouts  1.3 us

profile of v3, /device:TPU:16, one launch (start us, length us, event | category | flops | bytes accessed | tf_op | source)
XLA Modules:
  0.0 31.5 jit_solution(3135182918989597379)
XLA Ops:
  1.3 28.9 %shard_map.46 = f32[1,1,4,4,128]{4,3,2,1,0:T(4,128)} custom-call(f32[3,32,128,128]{3,2,1,0:T(8,128)} %vel.1, s32[4,1,16]{2,1,0:T(1,128)} %bitcast.7, f32[1,1]{1,0:T(1,128)} %bitcast.5.q_floor_in, f32[1,1]{1,0:T(1,128)} %bitcast.6.q_span_in), custom_call_target="tpu_custom_call" | custom-call | tf_op jit(solution)/shard_map/pallas_call | solution.py:326
  30.2 1.3 %copy.9 = f32[1,1,4,4,128]{4,3,2,1,0:T(4,128)} copy(f32[1,1,4,4,128]{4,3,2,1,0:T(4,128)} %shard_map.46) | data formatting | bytes 16384

commit v4 on v3

--- a/solution.py
+++ b/solution.py
@@ -13,6 +13,8 @@
 LANES = 128
 ROWS = 4
 VIEW = 8
+CHUNKS = 4
+CUT = 128 // CHUNKS
 
 
 def stencil(a, b, c, d):
@@ -38,12 +40,12 @@
     y_next, y_prev = lax.rem(gy + 1, n_gy), lax.rem(gy + n_gy - 1, n_gy)
 
     loads = []
-    for g in range(2):
+    for j in range(CHUNKS):
         for c in range(3):
             load = pltpu.make_async_copy(
-                vel.at[c, pl.ds(16 * g, 16)],
-                cells.at[c, pl.ds(2 + 16 * g, 16), pl.ds(8, 128)],
-                load_sem.at[g, c],
+                vel.at[c, :, pl.ds(CUT * j, CUT)],
+                cells.at[c, pl.ds(2, 32), pl.ds(8 + CUT * j, CUT)],
+                load_sem.at[j, c],
             )
             load.start()
             loads.append(load)
@@ -88,25 +90,18 @@
     lane = lax.broadcasted_iota(jnp.int32, (16, LANES), 1)
     pair_of = (lane % 8) // 2
 
-    def pack(g):
-        @pl.loop(0, 8)
-        def _(t):
-            rows = pl.ds(pl.multiple_of(8 + 16 * t, 8), 16)
-            own = pl.ds(pl.multiple_of(16 * t, 16), 16)
+    def pack(j):
+        @pl.loop(0, CUT // 8)
+        def _(q):
+            g, t = q % 2, q // 2
+            rows = pl.ds(pl.multiple_of(8 + CUT * j + 16 * t, 8), 16)
+            own = pl.ds(pl.multiple_of(CUT * j + 16 * t, 16), 16)
             gathered = [jnp.zeros((16, LANES), f32) for s in range(4)]
             for k in range(4):
                 for c in range(3):
                     here = lane // 8 == 4 * k + c
                     for s in range(4):
-                        x = 16 * g + 4 * s + k
-                        u = cells[c, 2 + x, rows]
-                        high = u.astype(bf16)
-                        rest = u - high.astype(f32)
-                        mid = rest.astype(bf16)
-                        low = (rest - mid.astype(f32)).astype(bf16)
-                        pieces[c, x, own, pl.ds(0, LANES)] = high
-                        pieces[c, x, own, pl.ds(LANES, LANES)] = mid
-                        pieces[c, x, own, pl.ds(2 * LANES, LANES)] = low
+                        u = cells[c, 2 + 16 * g + 4 * s + k, rows]
                         moved = pltpu.roll(u, (32 * k + 8 * c + 4) % LANES, 1)
                         gathered[s] = jnp.where(here, moved, gathered[s])
             left = right = None
@@ -138,27 +133,48 @@
         send_halo(3, vel.at[:, :, pl.ds(126, 2)], cells.at[:, pl.ds(2, 32), pl.ds(6, 2)], {"gy": y_next})
 
     z_copies = []
-    for g in range(2):
-        for c in range(3):
-            loads[3 * g + c].wait()
-        pack(g)
-        if g == 0:
+    for j in range(CHUNKS):
+        for c in range(3):
+            loads[3 * j + c].wait()
+        pack(j)
+        if j == 0:
             enter()
+        part = pl.ds(CUT * j, CUT)
         for side, (src, dst, step) in enumerate(((send_l, recv_l, -1), (send_r, recv_r, 1))):
             copy = pltpu.make_async_remote_copy(
-                src_ref=src.at[g], dst_ref=dst.at[g], send_sem=z_send.at[g, side],
-                recv_sem=z_recv.at[g, side], device_id={"view": view(step)}, device_id_type=MESH,
+                src_ref=src.at[:, part], dst_ref=dst.at[:, part], send_sem=z_send.at[j, side],
+                recv_sem=z_recv.at[j, side], device_id={"view": view(step)}, device_id_type=MESH,
             )
             copy.start()
             z_copies.append(copy)
 
-    for g in range(2):
-        for copy in z_copies[2 * g : 2 * g + 2]:
+    @pl.loop(0, 32)
+    def _(x):
+        for c in range(3):
+            for t in range(8):
+                own = pl.ds(16 * t, 16)
+                u = cells[c, 2 + x, pl.ds(8 + 16 * t, 16)]
+                high = u.astype(bf16)
+                rest = u - high.astype(f32)
+                mid = rest.astype(bf16)
+                low = (rest - mid.astype(f32)).astype(bf16)
+                pieces[c, x, own, pl.ds(0, LANES)] = high
+                pieces[c, x, own, pl.ds(LANES, LANES)] = mid
+                pieces[c, x, own, pl.ds(2 * LANES, LANES)] = low
+
+    for j in range(CHUNKS):
+        for copy in z_copies[2 * j : 2 * j + 2]:
             copy.wait_recv()
-
-        @pl.loop(0, 8)
-        def _(t):
-            own = pl.ds(pl.multiple_of(16 * t, 16), 16)
+        if j == 0:
+            for step in (2, -2):
+                pl.semaphore_signal(
+                    ready, inc=1, device_id={"view": view(step)}, device_id_type=MESH
+                )
+
+        @pl.loop(0, CUT // 8)
+        def _(q):
+            g, t = q % 2, q // 2
+            own = pl.ds(pl.multiple_of(CUT * j + 16 * t, 16), 16)
             after, before = recv_l[g, own], recv_r[g, own]
             for s in range(4):
                 both = jnp.where(pair_of == s, after, before)
@@ -170,9 +186,6 @@
                     placed = pltpu.roll(halo, (2 - 32 * k - 2 * s) % LANES, 1).astype(bf16)
                     for c in range(3):
                         pieces[c, 16 * g + 4 * s + k, own, pl.ds(3 * LANES, LANES)] = placed
-
-    for step in (2, -2):
-        pl.semaphore_signal(ready, inc=1, device_id={"view": view(step)}, device_id_type=MESH)
 
     for copy in halos[2:]:
         copy.wait_recv()
@@ -261,8 +274,6 @@
         def _():
             arrived[v] = parts[b]
 
-    pl.semaphore_wait(ready, 2)
-
     turn_depth(1, 1)
     levels(1, 1)
 
@@ -274,6 +285,10 @@
         turn_depth(2 * b + 1, 1)
         finish(2 * b, 0)
         levels(2 * b + 1, 1)
+
+        @pl.when(b == 2)
+        def _():
+            pl.semaphore_wait(ready, 2)
 
         @pl.when(b > 1)
         def _():
@@ -341,11 +356,11 @@
             pltpu.VMEM((256, 256), bf16),
             pltpu.VMEM((VIEW, 16, LANES), f32),
             pltpu.VMEM((VIEW, 16, LANES), f32),
-            pltpu.SemaphoreType.DMA((2, 3)),
+            pltpu.SemaphoreType.DMA((CHUNKS, 3)),
             pltpu.SemaphoreType.DMA((4,)),
             pltpu.SemaphoreType.DMA((4,)),
-            pltpu.SemaphoreType.DMA((2, 2)),
-            pltpu.SemaphoreType.DMA((2, 2)),
+            pltpu.SemaphoreType.DMA((CHUNKS, 2)),
+            pltpu.SemaphoreType.DMA((CHUNKS, 2)),
             pltpu.SemaphoreType.DMA((VIEW,)),
             pltpu.SemaphoreType.DMA((VIEW,)),
             pltpu.SemaphoreType.REGULAR,

time: 31.6 us -> 29.4 us (0.930)
  Pallas kernels: 28.9 us -> 26.6 us
    pallas_call x1, Pallas kernels: 28.9 us -> 26.6 us  [local(): pl.pallas_call(kernel, out_shape=jax.ShapeDtypeStruct((1, 1, 4, ROWS, LAN...]
where the time goes in v4:
time: 29.4 us; the launch traced here: 29.2 us
  Pallas kernels  26.6 us (90%)
  local copies, waits for them, and re-layouts  1.3 us (4%)
  between operations  1.3 us (4%)
    pallas_call x1, Pallas kernels, local(): pl.pallas_call(kernel, out_shape=jax.ShapeDtypeStruct((1, 1, 4, ROWS, LAN...  26.6 us
    unnamed x1, local copies, waits for them, and re-layouts  1.3 us

profile of v4, /device:TPU:16, one launch (start us, length us, event | category | flops | bytes accessed | tf_op | source)
XLA Modules:
  0.0 29.2 jit_solution(4562893331661848774)
XLA Ops:
  1.3 26.6 %shard_map.46 = f32[1,1,4,4,128]{4,3,2,1,0:T(4,128)} custom-call(f32[3,32,128,128]{3,2,1,0:T(8,128)} %vel.1, s32[4,1,16]{2,1,0:T(1,128)} %bitcast.7, f32[1,1]{1,0:T(1,128)} %bitcast.5.q_floor_in, f32[1,1]{1,0:T(1,128)} %bitcast.6.q_span_in), custom_call_target="tpu_custom_call" | custom-call | tf_op jit(solution)/shard_map/pallas_call | solution.py:341
  27.9 1.3 %copy.9 = f32[1,1,4,4,128]{4,3,2,1,0:T(4,128)} copy(f32[1,1,4,4,128]{4,3,2,1,0:T(4,128)} %shard_map.46) | data formatting | bytes 16384

commit v5 on v4

--- a/solution.py
+++ b/solution.py
@@ -91,26 +91,26 @@
     pair_of = (lane % 8) // 2
 
     def pack(j):
-        @pl.loop(0, CUT // 8)
-        def _(q):
-            g, t = q % 2, q // 2
+        @pl.loop(0, CUT // 16)
+        def _(t):
             rows = pl.ds(pl.multiple_of(8 + CUT * j + 16 * t, 8), 16)
             own = pl.ds(pl.multiple_of(CUT * j + 16 * t, 16), 16)
-            gathered = [jnp.zeros((16, LANES), f32) for s in range(4)]
-            for k in range(4):
-                for c in range(3):
-                    here = lane // 8 == 4 * k + c
-                    for s in range(4):
-                        u = cells[c, 2 + 16 * g + 4 * s + k, rows]
-                        moved = pltpu.roll(u, (32 * k + 8 * c + 4) % LANES, 1)
-                        gathered[s] = jnp.where(here, moved, gathered[s])
-            left = right = None
-            for s in range(4):
-                turned = gathered[s] if s == 2 else pltpu.roll(gathered[s], (2 * s - 4) % LANES, 1)
-                left = turned if s == 0 else jnp.where(pair_of == s, turned, left)
-                right = turned if s == 0 else jnp.where(pair_of == (s + 3) % 4, turned, right)
-            send_l[g, own] = left
-            send_r[g, own] = right
+            for g in range(2):
+                gathered = [jnp.zeros((16, LANES), f32) for s in range(4)]
+                for k in range(4):
+                    for c in range(3):
+                        here = lane // 8 == 4 * k + c
+                        for s in range(4):
+                            u = cells[c, 2 + 16 * g + 4 * s + k, rows]
+                            moved = pltpu.roll(u, (32 * k + 8 * c + 4) % LANES, 1)
+                            gathered[s] = jnp.where(here, moved, gathered[s])
+                left = right = None
+                for s in range(4):
+                    turned = gathered[s] if s == 2 else pltpu.roll(gathered[s], (2 * s - 4) % LANES, 1)
+                    left = turned if s == 0 else jnp.where(pair_of == s, turned, left)
+                    right = turned if s == 0 else jnp.where(pair_of == (s + 3) % 4, turned, right)
+                send_l[g, own] = left
+                send_r[g, own] = right
 
     halos = []
 
@@ -127,18 +127,18 @@
             halos.append(copy)
 
         body = pl.ds(8, 128)
-        send_halo(0, vel.at[:, pl.ds(0, 2)], cells.at[:, pl.ds(34, 2), body], {"gx": x_prev})
-        send_halo(1, vel.at[:, pl.ds(30, 2)], cells.at[:, pl.ds(0, 2), body], {"gx": x_next})
+        send_halo(0, vel.at[:, pl.ds(30, 2)], cells.at[:, pl.ds(0, 2), body], {"gx": x_next})
+        send_halo(1, vel.at[:, pl.ds(0, 2)], cells.at[:, pl.ds(34, 2), body], {"gx": x_prev})
         send_halo(2, vel.at[:, :, pl.ds(0, 2)], cells.at[:, pl.ds(2, 32), pl.ds(136, 2)], {"gy": y_prev})
         send_halo(3, vel.at[:, :, pl.ds(126, 2)], cells.at[:, pl.ds(2, 32), pl.ds(6, 2)], {"gy": y_next})
 
+    enter()
+
     z_copies = []
     for j in range(CHUNKS):
         for c in range(3):
             loads[3 * j + c].wait()
         pack(j)
-        if j == 0:
-            enter()
         part = pl.ds(CUT * j, CUT)
         for side, (src, dst, step) in enumerate(((send_l, recv_l, -1), (send_r, recv_r, 1))):
             copy = pltpu.make_async_remote_copy(
@@ -277,7 +277,7 @@
     turn_depth(1, 1)
     levels(1, 1)
 
-    @pl.loop(1, VIEW - 1)
+    @pl.loop(1, VIEW - 2)
     def _(b):
         turn_depth(2 * b, 0)
         finish(2 * b - 1, 1)
@@ -294,20 +294,28 @@
         def _():
             hand_over(b - 1)
 
-    turn_depth(14, 0)
-    finish(13, 1)
-    levels(14, 0)
+    turn_depth(0, 0)
+    finish(11, 1)
+    hand_over(5)
+
+    halos[0].wait_recv()
+    levels(0, 0)
+    finish(0, 0)
+    hand_over(0)
+
+    turn_depth(12, 1)
+    levels(12, 1)
+    turn_depth(13, 0)
+    finish(12, 1)
+    levels(13, 0)
+    turn_depth(14, 1)
+    finish(13, 0)
     hand_over(6)
-    turn_depth(0, 1)
-    finish(14, 0)
+    levels(14, 1)
     turn_depth(15, 0)
-
-    for copy in halos[:2]:
-        copy.wait_recv()
-
-    levels(0, 1)
-    finish(0, 1)
-    hand_over(0)
+    finish(14, 1)
+
+    halos[1].wait_recv()
     levels(15, 0)
     finish(15, 0)
     hand_over(7)

time: 29.4 us -> 28.4 us (0.966)
  Pallas kernels: 26.6 us -> 25.7 us
    pallas_call x1, Pallas kernels: 26.6 us -> 25.7 us  [local(): pl.pallas_call(kernel, out_shape=jax.ShapeDtypeStruct((1, 1, 4, ROWS, LAN...]
where the time goes in v5:
time: 28.4 us; the launch traced here: 28.3 us
  Pallas kernels  25.7 us (90%)
  local copies, waits for them, and re-layouts  1.3 us (5%)
  between operations  1.3 us (5%)
    pallas_call x1, Pallas kernels, local(): pl.pallas_call(kernel, out_shape=jax.ShapeDtypeStruct((1, 1, 4, ROWS, LAN...  25.7 us
    unnamed x1, local copies, waits for them, and re-layouts  1.3 us

profile of v5, /device:TPU:16, one launch (start us, length us, event | category | flops | bytes accessed | tf_op | source)
XLA Modules:
  0.0 28.3 jit_solution(12651723982944348468)
XLA Ops:
  1.3 25.7 %shard_map.46 = f32[1,1,4,4,128]{4,3,2,1,0:T(4,128)} custom-call(f32[3,32,128,128]{3,2,1,0:T(8,128)} %vel.1, s32[4,1,16]{2,1,0:T(1,128)} %bitcast.7, f32[1,1]{1,0:T(1,128)} %bitcast.5.q_floor_in, f32[1,1]{1,0:T(1,128)} %bitcast.6.q_span_in), custom_call_target="tpu_custom_call" | custom-call | tf_op jit(solution)/shard_map/pallas_call | solution.py:349
  27.0 1.3 %copy.9 = f32[1,1,4,4,128]{4,3,2,1,0:T(4,128)} copy(f32[1,1,4,4,128]{4,3,2,1,0:T(4,128)} %shard_map.46) | data formatting | bytes 16384

commit v6 on v5

--- a/solution.py
+++ b/solution.py
@@ -39,6 +39,13 @@
     x_next, x_prev = lax.rem(gx + 1, n_gx), lax.rem(gx + n_gx - 1, n_gx)
     y_next, y_prev = lax.rem(gy + 1, n_gy), lax.rem(gy + n_gy - 1, n_gy)
 
+    barrier = pltpu.get_barrier_semaphore()
+    for target in (
+        {"gx": x_next}, {"gx": x_prev}, {"gy": y_next}, {"gy": y_prev},
+        {"view": view(1)}, {"view": view(-1)},
+    ):
+        pl.semaphore_signal(barrier, inc=1, device_id=target, device_id_type=MESH)
+
     loads = []
     for j in range(CHUNKS):
         for c in range(3):
@@ -55,13 +62,6 @@
         copy = pltpu.make_async_copy(src, dst, small_sem.at[n])
         copy.start()
         small.append(copy)
-
-    barrier = pltpu.get_barrier_semaphore()
-    for target in (
-        {"gx": x_next}, {"gx": x_prev}, {"gy": y_next}, {"gy": y_prev},
-        {"view": view(1)}, {"view": view(-1)},
-    ):
-        pl.semaphore_signal(barrier, inc=1, device_id=target, device_id_type=MESH)
 
     row_id = lax.broadcasted_iota(jnp.int32, (256, 256), 0)
     col_id = lax.broadcasted_iota(jnp.int32, (256, 256), 1)
@@ -114,23 +114,30 @@
 
     halos = []
 
+    def send_halo(number, src, dst, target):
+        copy = pltpu.make_async_remote_copy(
+            src_ref=src, dst_ref=dst, send_sem=halo_send.at[number], recv_sem=halo_recv.at[number],
+            device_id=target, device_id_type=MESH,
+        )
+        copy.start()
+        halos.append(copy)
+
     def enter():
         pl.semaphore_wait(barrier, 6)
 
 
-        def send_halo(number, src, dst, target):
-            copy = pltpu.make_async_remote_copy(
-                src_ref=src, dst_ref=dst, send_sem=halo_send.at[number], recv_sem=halo_recv.at[number],
-                device_id=target, device_id_type=MESH,
+        for n in range(2):
+            half = pl.ds(64 * n, 64)
+            send_halo(
+                n, vel.at[:, pl.ds(30, 2), half],
+                cells.at[:, pl.ds(0, 2), pl.ds(8 + 64 * n, 64)], {"gx": x_next},
             )
-            copy.start()
-            halos.append(copy)
-
-        body = pl.ds(8, 128)
-        send_halo(0, vel.at[:, pl.ds(30, 2)], cells.at[:, pl.ds(0, 2), body], {"gx": x_next})
-        send_halo(1, vel.at[:, pl.ds(0, 2)], cells.at[:, pl.ds(34, 2), body], {"gx": x_prev})
-        send_halo(2, vel.at[:, :, pl.ds(0, 2)], cells.at[:, pl.ds(2, 32), pl.ds(136, 2)], {"gy": y_prev})
-        send_halo(3, vel.at[:, :, pl.ds(126, 2)], cells.at[:, pl.ds(2, 32), pl.ds(6, 2)], {"gy": y_next})
+        send_halo(
+            2, vel.at[:, :, pl.ds(0, 2)], cells.at[:, pl.ds(2, 32), pl.ds(136, 2)], {"gy": y_prev}
+        )
+        send_halo(
+            3, vel.at[:, :, pl.ds(126, 2)], cells.at[:, pl.ds(2, 32), pl.ds(6, 2)], {"gy": y_next}
+        )
 
     enter()
 
@@ -161,6 +168,10 @@
                 pieces[c, x, own, pl.ds(0, LANES)] = high
                 pieces[c, x, own, pl.ds(LANES, LANES)] = mid
                 pieces[c, x, own, pl.ds(2 * LANES, LANES)] = low
+
+    send_halo(
+        4, vel.at[:, pl.ds(0, 2)], cells.at[:, pl.ds(34, 2), pl.ds(8, 128)], {"gx": x_prev}
+    )
 
     for j in range(CHUNKS):
         for copy in z_copies[2 * j : 2 * j + 2]:
@@ -187,7 +198,7 @@
                     for c in range(3):
                         pieces[c, 16 * g + 4 * s + k, own, pl.ds(3 * LANES, LANES)] = placed
 
-    for copy in halos[2:]:
+    for copy in halos[2:4]:
         copy.wait_recv()
 
     for copy in small:
@@ -227,9 +238,9 @@
                 preferred_element_type=f32,
             )
 
-    def levels(p, odd):
+    def levels(p, odd, tiles=range(8)):
         for k in range(2):
-            for t in range(8):
+            for t in tiles:
                 lev = level_of(p, odd, k, t)
                 high = lev.astype(bf16)
                 low = (lev - high.astype(f32)).astype(bf16)
@@ -274,17 +285,20 @@
         def _():
             arrived[v] = parts[b]
 
+    def two_pairs(p):
+        turn_depth(p, 0)
+        finish(p - 1, 1)
+        levels(p, 0)
+        turn_depth(p + 1, 1)
+        finish(p, 0)
+        levels(p + 1, 1)
+
     turn_depth(1, 1)
     levels(1, 1)
 
-    @pl.loop(1, VIEW - 2)
+    @pl.loop(1, 5)
     def _(b):
-        turn_depth(2 * b, 0)
-        finish(2 * b - 1, 1)
-        levels(2 * b, 0)
-        turn_depth(2 * b + 1, 1)
-        finish(2 * b, 0)
-        levels(2 * b + 1, 1)
+        two_pairs(2 * b)
 
         @pl.when(b == 2)
         def _():
@@ -295,27 +309,26 @@
             hand_over(b - 1)
 
     turn_depth(0, 0)
-    finish(11, 1)
-    hand_over(5)
-
-    halos[0].wait_recv()
-    levels(0, 0)
+    finish(9, 1)
+    hand_over(4)
+
+    for n in range(2):
+        halos[n].wait_recv()
+        levels(0, 0, range(4 * n, 4 * n + 4))
     finish(0, 0)
     hand_over(0)
 
-    turn_depth(12, 1)
-    levels(12, 1)
-    turn_depth(13, 0)
-    finish(12, 1)
-    levels(13, 0)
-    turn_depth(14, 1)
-    finish(13, 0)
-    hand_over(6)
-    levels(14, 1)
+    turn_depth(10, 1)
+    levels(10, 1)
+
+    @pl.loop(5, 7)
+    def _(b):
+        two_pairs(2 * b + 1)
+        hand_over(b)
+
     turn_depth(15, 0)
     finish(14, 1)
-
-    halos[1].wait_recv()
+    halos[4].wait_recv()
     levels(15, 0)
     finish(15, 0)
     hand_over(7)
@@ -365,8 +378,8 @@
             pltpu.VMEM((VIEW, 16, LANES), f32),
             pltpu.VMEM((VIEW, 16, LANES), f32),
             pltpu.SemaphoreType.DMA((CHUNKS, 3)),
-            pltpu.SemaphoreType.DMA((4,)),
-            pltpu.SemaphoreType.DMA((4,)),
+            pltpu.SemaphoreType.DMA((5,)),
+            pltpu.SemaphoreType.DMA((5,)),
             pltpu.SemaphoreType.DMA((CHUNKS, 2)),
             pltpu.SemaphoreType.DMA((CHUNKS, 2)),
             pltpu.SemaphoreType.DMA((VIEW,)),

time: 28.4 us -> 27.7 us (0.975)
  Pallas kernels: 25.7 us -> 25 us
    pallas_call x1, Pallas kernels: 25.7 us -> 25 us  [local(): pl.pallas_call(kernel, out_shape=jax.ShapeDtypeStruct((1, 1, 4, ROWS, LAN...]
where the time goes in v6:
time: 27.7 us; the launch traced here: 27.6 us
  Pallas kernels  25 us (90%)
  local copies, waits for them, and re-layouts  1.3 us (5%)
  between operations  1.3 us (5%)
    pallas_call x1, Pallas kernels, local(): pl.pallas_call(kernel, out_shape=jax.ShapeDtypeStruct((1, 1, 4, ROWS, LAN...  25 us
    unnamed x1, local copies, waits for them, and re-layouts  1.3 us

profile of v6, /device:TPU:16, one launch (start us, length us, event | category | flops | bytes accessed | tf_op | source)
XLA Modules:
  0.0 27.6 jit_solution(15010948405996353765)
XLA Ops:
  1.3 25.0 %shard_map.46 = f32[1,1,4,4,128]{4,3,2,1,0:T(4,128)} custom-call(f32[3,32,128,128]{3,2,1,0:T(8,128)} %vel.1, s32[4,1,16]{2,1,0:T(1,128)} %bitcast.7, f32[1,1]{1,0:T(1,128)} %bitcast.5.q_floor_in, f32[1,1]{1,0:T(1,128)} %bitcast.6.q_span_in), custom_call_target="tpu_custom_call" | custom-call | tf_op jit(solution)/shard_map/pallas_call | solution.py:362
  26.3 1.3 %copy.9 = f32[1,1,4,4,128]{4,3,2,1,0:T(4,128)} copy(f32[1,1,4,4,128]{4,3,2,1,0:T(4,128)} %shard_map.46) | data formatting | bytes 16384

commit v7 on v6

--- a/solution.py
+++ b/solution.py
@@ -296,7 +296,7 @@
     turn_depth(1, 1)
     levels(1, 1)
 
-    @pl.loop(1, 5)
+    @pl.loop(1, 4)
     def _(b):
         two_pairs(2 * b)
 
@@ -309,8 +309,8 @@
             hand_over(b - 1)
 
     turn_depth(0, 0)
-    finish(9, 1)
-    hand_over(4)
+    finish(7, 1)
+    hand_over(3)
 
     for n in range(2):
         halos[n].wait_recv()
@@ -318,10 +318,10 @@
     finish(0, 0)
     hand_over(0)
 
-    turn_depth(10, 1)
-    levels(10, 1)
-
-    @pl.loop(5, 7)
+    turn_depth(8, 1)
+    levels(8, 1)
+
+    @pl.loop(4, 7)
     def _(b):
         two_pairs(2 * b + 1)
         hand_over(b)

time: 27.7 us -> 27.2 us (0.982)
  Pallas kernels: 25 us -> 24.3 us
    pallas_call x1, Pallas kernels: 25 us -> 24.3 us  [local(): pl.pallas_call(kernel, out_shape=jax.ShapeDtypeStruct((1, 1, 4, ROWS, LAN...]
where the time goes in v7:
time: 27.2 us; the launch traced here: 26.9 us
  Pallas kernels  24.3 us (89%)
  local copies, waits for them, and re-layouts  1.3 us (5%)
  between operations  1.3 us (5%)
    pallas_call x1, Pallas kernels, local(): pl.pallas_call(kernel, out_shape=jax.ShapeDtypeStruct((1, 1, 4, ROWS, LAN...  24.3 us
    unnamed x1, local copies, waits for them, and re-layouts  1.3 us

profile of v7, /device:TPU:16, one launch (start us, length us, event | category | flops | bytes accessed | tf_op | source)
XLA Modules:
  0.0 26.9 jit_solution(10798538017796962095)
XLA Ops:
  1.3 24.3 %shard_map.46 = f32[1,1,4,4,128]{4,3,2,1,0:T(4,128)} custom-call(f32[3,32,128,128]{3,2,1,0:T(8,128)} %vel.1, s32[4,1,16]{2,1,0:T(1,128)} %bitcast.7, f32[1,1]{1,0:T(1,128)} %bitcast.5.q_floor_in, f32[1,1]{1,0:T(1,128)} %bitcast.6.q_span_in), custom_call_target="tpu_custom_call" | custom-call | tf_op jit(solution)/shard_map/pallas_call | solution.py:362
  25.6 1.3 %copy.9 = f32[1,1,4,4,128]{4,3,2,1,0:T(4,128)} copy(f32[1,1,4,4,128]{4,3,2,1,0:T(4,128)} %shard_map.46) | data formatting | bytes 16384

commit v8 on v7

--- a/solution.py
+++ b/solution.py
@@ -22,10 +22,10 @@
 
 
 def kernel(
-    vel, occ_in, q_floor_in, q_span_in, out,
+    vel, occ_in, q_floor, q_span, out,
     cells, pieces, stencils, send_l, send_r, recv_l, recv_r, deep_ref, split, lower, parts, arrived,
     load_sem, halo_send, halo_recv, z_send, z_recv, part_send, part_recv, ready,
-    occ, q_floor, q_span, small_sem,
+    occ, small_sem,
 ):
     f32, bf16 = jnp.float32, jnp.bfloat16
     v = lax.axis_index("view")
@@ -58,7 +58,7 @@
             loads.append(load)
 
     small = []
-    for n, (src, dst) in enumerate(((occ_in, occ), (q_floor_in, q_floor), (q_span_in, q_span))):
+    for n, (src, dst) in enumerate(((occ_in, occ),)):
         copy = pltpu.make_async_copy(src, dst, small_sem.at[n])
         copy.start()
         small.append(copy)
@@ -205,8 +205,8 @@
         copy.wait()
 
     unit = -(5.0 / (LANES * VIEW)) * math.log2(math.e)
-    slope = -unit / (4.5 * q_span[0, 0])
-    shift = -unit * q_floor[0, 0] / q_span[0, 0]
+    slope = -unit / (4.5 * q_span[0])
+    shift = -unit * q_floor[0] / q_span[0]
 
     def level_of(p, odd, k, t):
         x = 2 * p + k + 2
@@ -361,8 +361,8 @@
     here = pl.BlockSpec(memory_space=pltpu.HBM)
     return pl.pallas_call(
         kernel,
-        out_shape=jax.ShapeDtypeStruct((1, 1, 4, ROWS, LANES), f32),
-        in_specs=[here] * 4,
+        out_shape=pltpu.VMEM((1, 1, 4, ROWS, LANES), f32),
+        in_specs=[here, here] + [pl.BlockSpec(memory_space=pltpu.SMEM)] * 2,
         out_specs=pl.BlockSpec(memory_space=pltpu.VMEM),
         scratch_shapes=[
             pltpu.VMEM((3, 36, 144, LANES), f32),
@@ -386,12 +386,10 @@
             pltpu.SemaphoreType.DMA((VIEW,)),
             pltpu.SemaphoreType.REGULAR,
             pltpu.SMEM((4, 1, 16), jnp.int32),
-            pltpu.SMEM((1, 1), f32),
-            pltpu.SMEM((1, 1), f32),
             pltpu.SemaphoreType.DMA((3,)),
         ],
         compiler_params=pltpu.CompilerParams(collective_id=0, has_side_effects=True),
-    )(velocity, occupied.transpose(0, 2, 1), q_floor.reshape(1, 1), q_span.reshape(1, 1))
+    )(velocity, occupied.transpose(0, 2, 1), q_floor, q_span)
 
 
 def solution(mesh):

time: 27.2 us -> 25.8 us (0.949)
  local copies, waits for them, and re-layouts: 1.3 us -> 0.6 us
  Pallas kernels: 24.3 us -> 23.7 us
    unnamed x1, local copies, waits for them, and re-layouts: 1.3 us -> 0.6 us
    pallas_call x1, Pallas kernels: 24.3 us -> 23.7 us  [local(): pl.pallas_call(kernel, out_shape=pltpu.VMEM((1, 1, 4, ROWS, LANES), f32),...]
where the time goes in v8:
time: 25.8 us; the launch traced here: 25.6 us
  Pallas kernels  23.7 us (92%)
  between operations  1.3 us (5%)
  local copies, waits for them, and re-layouts  0.6 us (2%)
    pallas_call x1, Pallas kernels, local(): pl.pallas_call(kernel, out_shape=pltpu.VMEM((1, 1, 4, ROWS, LANES), f32),...  23.7 us
    unnamed x1, local copies, waits for them, and re-layouts  0.6 us

profile of v8, /device:TPU:16, one launch (start us, length us, event | category | flops | bytes accessed | tf_op | source)
XLA Modules:
  0.0 25.6 jit_solution(15561874571440022984)
XLA Ops:
  1.3 23.7 %shard_map.46 = f32[1,1,4,4,128]{4,3,2,1,0:T(4,128)S(1)} custom-call(f32[3,32,128,128]{3,2,1,0:T(8,128)} %vel.1, s32[4,1,16]{2,1,0:T(1,128)} %bitcast.3, f32[1]{0:T(128)S(6)} %copy.8.q_floor, f32[1]{0:T(128)S(6)} %copy.9.q_span), custom_call_target="tpu_custom_call" | custom-call | tf_op jit(solution)/shard_map/pallas_call | solution.py:362
  25.0 0.6 %copy.7 = f32[1,1,4,4,128]{4,3,2,1,0:T(4,128)} copy(f32[1,1,4,4,128]{4,3,2,1,0:T(4,128)S(1)} %shard_map.46) | data formatting | bytes 16384

commit v9 on v8

--- a/solution.py
+++ b/solution.py
@@ -155,6 +155,10 @@
             copy.start()
             z_copies.append(copy)
 
+    send_halo(
+        4, vel.at[:, pl.ds(0, 2)], cells.at[:, pl.ds(34, 2), pl.ds(8, 128)], {"gx": x_prev}
+    )
+
     @pl.loop(0, 32)
     def _(x):
         for c in range(3):
@@ -168,10 +172,6 @@
                 pieces[c, x, own, pl.ds(0, LANES)] = high
                 pieces[c, x, own, pl.ds(LANES, LANES)] = mid
                 pieces[c, x, own, pl.ds(2 * LANES, LANES)] = low
-
-    send_halo(
-        4, vel.at[:, pl.ds(0, 2)], cells.at[:, pl.ds(34, 2), pl.ds(8, 128)], {"gx": x_prev}
-    )
 
     for j in range(CHUNKS):
         for copy in z_copies[2 * j : 2 * j + 2]:
@@ -333,6 +333,10 @@
     finish(15, 0)
     hand_over(7)
 
+    for copy in halos + z_copies:
+        copy.wait_send()
+    for step in range(1, VIEW):
+        part_copy(view(step), v).wait_send()
     for step in range(1, VIEW):
         part_copy(view(step), view(step)).wait_recv()
 
@@ -349,11 +353,6 @@
     out[0, 0, 1] = green
     out[0, 0, 2] = (1.0 - ahead) - red
     out[0, 0, 3] = 1.0 - ahead
-
-    for copy in halos + z_copies:
-        copy.wait_send()
-    for step in range(1, VIEW):
-        part_copy(view(step), v).wait_send()
 
 
 def local(velocity, occupied, q_floor, q_span):

time: 25.8 us -> 25.8 us (level)
  no operation moved by 1% of the time
where the time goes in v9:
time: 25.8 us; the launch traced here: 25.5 us
  Pallas kernels  23.6 us (91%)
  between operations  1.3 us (5%)
  local copies, waits for them, and re-layouts  0.6 us (2%)
    pallas_call x1, Pallas kernels, local(): pl.pallas_call(kernel, out_shape=pltpu.VMEM((1, 1, 4, ROWS, LANES), f32),...  23.6 us
    unnamed x1, local copies, waits for them, and re-layouts  0.6 us

profile of v9, /device:TPU:16, one launch (start us, length us, event | category | flops | bytes accessed | tf_op | source)
XLA Modules:
  0.0 25.5 jit_solution(12465500737037695814)
XLA Ops:
  1.3 23.6 %shard_map.46 = f32[1,1,4,4,128]{4,3,2,1,0:T(4,128)S(1)} custom-call(f32[3,32,128,128]{3,2,1,0:T(8,128)} %vel.1, s32[4,1,16]{2,1,0:T(1,128)} %bitcast.3, f32[1]{0:T(128)S(6)} %copy.8.q_floor, f32[1]{0:T(128)S(6)} %copy.9.q_span), custom_call_target="tpu_custom_call" | custom-call | tf_op jit(solution)/shard_map/pallas_call | solution.py:361
  24.9 0.6 %copy.7 = f32[1,1,4,4,128]{4,3,2,1,0:T(4,128)} copy(f32[1,1,4,4,128]{4,3,2,1,0:T(4,128)S(1)} %shard_map.46) | data formatting | bytes 16384
